TPU v7x, 32 devices: a whole 2x2x4 slice. The times are simulated.
32 devices in a mesh: shot: 32 (over z, y, x, core), freq: 1.
Axes of the slice: x: 2, y: 2, z: 4, core: 2. Of those that a mesh axis runs over, the one named last changes fastest.
Arguments:
- data: bfloat16 [2, 64, 128, 128], P(None, 'freq', 'shot')
- aperture: int32 [128, 64], P('shot'), may hold values from -1 to 127, as said below
- ops: bfloat16 [8, 64, 64], replicated, may hold values from -0.75 to 0.75
- cable_ops: int32 [2], replicated, may hold values from 0 to 7
Outputs:
- multiples: bfloat16 [2, 64, 128, 128], P(None, 'freq', 'shot')
Inputs may be any that keep to these rules, and one draw needn't show every extreme that they name: `aperture`: each shot's list holds 1 to 64 distinct surface points first, then -1 padding; some shot's list is full.
All inputs are finite; a program needn't handle non-finite values.
Results may differ from a plain program's by a relative error of at most 0.0004.
Values may be sent and summed in bfloat16 or wider, within the bound.
A program may use at most 64 MiB of HBM per device.

v0:
```python
import jax
import jax.numpy as jnp
from jax import lax
from jax.sharding import PartitionSpec as P


def cable_apply(field, chosen):
    shape = field.shape
    cables = chosen.shape[0]
    split = field.reshape(shape[0], shape[1], shape[2], cables, shape[3] // cables)
    result = jnp.einsum("pfsci,cij->pfscj", split, chosen, precision=lax.Precision.HIGHEST)
    return result.reshape(shape)


def complex_block(block, piece):

    def product(left_factor, right_factor):
        return jnp.einsum(
            "jpy,jyu->jpu", left_factor, right_factor, preferred_element_type=jnp.float32
        )

    real_part = product(block[0], piece[0]) - product(block[1], piece[1])
    imaginary_part = product(block[0], piece[1]) + product(block[1], piece[0])
    return jnp.stack([real_part, imaginary_part])


def make_mask(aperture, total):
    surface = lax.iota(jnp.int32, total)
    return jnp.any(aperture[:, :, None] == surface[None, None, :], axis=1).astype(jnp.bfloat16)


def per_device(data, aperture, ops, cable_ops):
    total = data.shape[3]
    op_count = ops.shape[0]
    onehot = (cable_ops[:, None] == lax.iota(jnp.int32, op_count)[None, :]).astype(jnp.float32)
    chosen = jnp.dot(
        onehot, ops.reshape(op_count, -1).astype(jnp.float32), precision=lax.Precision.HIGHEST
    )
    chosen = chosen.reshape(cable_ops.shape[0], ops.shape[1], ops.shape[2])
    all_freqs = data.shape[1] * lax.axis_size("freq")
    mask = make_mask(aperture, total)
    masked_wavefield = data * mask[None, None, :, :]
    partial_sum = complex_block(masked_wavefield, lax.all_gather(data, "shot", axis=2, tiled=True))
    predicted = cable_apply(partial_sum, chosen)
    local_energy = jnp.sum(predicted * predicted, axis=(0, 1, 3))
    energy = lax.psum(local_energy, "freq")
    scale = lax.rsqrt(energy / (2.0 * all_freqs * total) + 1e-06)
    return (predicted * scale[None, None, :, None]).astype(jnp.bfloat16)


def solution(mesh):
    return jax.shard_map(
        per_device,
        mesh=mesh,
        in_specs=(P(None, "freq", "shot", None), P("shot", None), P(), P()),
        out_specs=P(None, "freq", "shot", None),
        check_vma=False,
    )
```

profile of v0, /device:TPU:0, one launch (start us, length us, event | category | flops | bytes accessed | tf_op | source)
XLA Modules:
  0.0 95.8 jit_solution(15762430939821259372)
XLA Ops:
  6.5 0.0 all-gather.2.cloned.1.call-start
  6.5 1.6 %copy.29 = bf16[2,64,4,128]{3,1,0,2:T(8,128)(2,1)} copy(bf16[2,64,4,128]{3,2,1,0:T(4,128)(2,1)} %param.4) | data formatting | bytes 262144 | tf_op args[0]
  8.1 0.0 all-gather.2.cloned.1.call-update
  8.1 0.8 fusion.10
  8.9 1.1 %reshape.23 = bf16[8,4096]{1,0:T(8,128)(2,1)S(1)} reshape(bf16[8,64,64]{2,1,0:T(8,128)(2,1)} %param.6) | data formatting | bytes 131072 | tf_op jit(solution)/shard_map/reshape | solution.py:37
  10.0 0.2 dot_general.23
  10.2 0.9 convolution_bitcast_fusion.1
  11.1 0.9 broadcast_multiply_fusion
  12.0 62.6 %all-gather.2.cloned.1.call-done = bf16[2,64,128,128]{3,1,0,2:T(8,128)(2,1)} async-done(((bf16[2,64,4,128]{3,1,0,2:T(8,128)(2,1)}), bf16[2,64,128,128]{3,1,0,2:T(8,128)(2,1)}) %all-gather.2.cloned.1.call-update) | async-done | bytes 4194320 | tf_op jit(solution)/shard_map/all_gather | solution.py:43
  74.7 3.2 %fusion.17 = (bf16[1,64,128,128]{3,1,0,2:T(8,128)(2,1)S(1)}, bf16[1,64,128,128]{3,1,0,2:T(8,128)(2,1)S(1)}) fusion(bf16[2,64,128,128]{3,1,0,2:T(8,128)(2,1)} %all-gather.2.cloned.1.call-done), kind=kLoop, calls=%fused_computation.28 | loop fusion | bytes 8388608 | tf_op jit(solution)/shard_map/slice | solution.py:22
  77.9 1.8 %fusion = f32[64,4,128]{2,1,0:T(4,128)S(1)} fusion(bf16[1,64,128,128]{3,1,0,2:T(8,128)(2,1)S(1)} %get-tuple-element.6, bf16[2,64,4,128]{3,2,1,0:T(4,128)(2,1)S(1)} %bitcast.35), kind=kOutput, calls=%fused_computation.2 | convolution fusion | flops 8388608 | bytes 2293760 | tf_op jit(solution)/shard_map/jpy,jyu->jpu/dot_general | solution.py:18
  79.7 1.8 %fusion.1 = f32[64,4,128]{2,1,0:T(4,128)S(1)} fusion(bf16[1,64,128,128]{3,1,0,2:T(8,128)(2,1)S(1)} %get-tuple-element.6, bf16[2,64,4,128]{3,2,1,0:T(4,128)(2,1)S(1)} %bitcast.36), kind=kOutput, calls=%fused_computation.3 | convolution fusion | flops 8388608 | bytes 2293760 | tf_op jit(solution)/shard_map/jpy,jyu->jpu/dot_general | solution.py:18
  81.5 1.9 %fusion.5 = f32[64,4,128]{2,1,0:T(4,128)S(1)} fusion(f32[64,4,128]{2,1,0:T(4,128)S(1)} %fusion, bf16[1,64,128,128]{3,1,0,2:T(8,128)(2,1)S(1)} %get-tuple-element.5, bf16[2,64,4,128]{3,2,1,0:T(4,128)(2,1)S(1)} %bitcast.37), kind=kOutput, calls=%fused_computation.8 | convolution fusion | flops 8421376 | bytes 2424832 | tf_op jit(solution)/shard_map/jpy,jyu->jpu/dot_general | solution.py:18
  83.4 0.2 stack.10
  83.6 0.1 copy.33
  83.7 1.9 %fusion.4 = f32[64,4,128]{2,1,0:T(4,128)S(1)} fusion(f32[64,4,128]{2,1,0:T(4,128)S(1)} %fusion.1, bf16[1,64,128,128]{3,1,0,2:T(8,128)(2,1)S(1)} %get-tuple-element.5, bf16[2,64,4,128]{3,2,1,0:T(4,128)(2,1)S(1)} %bitcast.38), kind=kOutput, calls=%fused_computation.7 | convolution fusion | flops 8421376 | bytes 2424832 | tf_op jit(solution)/shard_map/jpy,jyu->jpu/dot_general | solution.py:18
  85.5 0.2 stack.9
  85.7 0.1 copy.32
  85.8 1.8 %multiply_reduce_fusion = (f32[4]{0:T(128)S(1)}, f32[2,64,4,2,64]{1,4,2,0,3:T(8,128)S(1)}) fusion(f32[1,64,4,2,64]{4,1,2,0,3:T(8,128)S(1)} %copy.33, f32[1,64,4,2,64]{4,1,2,0,3:T(8,128)S(1)} %copy.32, f32[2,64,64,1,1]{2,0,1,4,3:T(2,128)S(1)} %convolution_bitcast_fusion.1), kind=kOutput, calls=%fused_computation.13 | convolution fusion | flops 50528252 | bytes 557072 | tf_op jit(solution)/shard_map/pfsci,cij->pfscj/dot_general | solution.py:11
  87.5 0.3 copy.35
  87.8 0.3 reshape.24
  88.1 0.1 multiply_convert_fusion
  88.2 0.8 copy.36
  (3 shorter events, 0.0 us)
Async XLA Ops:
  6.5 68.1 %all-gather.2.cloned.1.call-start = ((), (), s32[]{:S(2)}) async-start(), calls=%async_computation | async-start | bytes 4325376 | tf_op jit(solution)/shard_map/all_gather | solution.py:43
Sparse Core Ops, SparseCore 0:
  10.2 64.4 all-gather.1
where the time goes:
time: 96 us; the launch traced here: 95.8 us
  waiting for transfers between devices  62.6 us (65%)
  between operations  13.5 us (14%)
  matrix products  10 us (10%)
  local copies, waits for them, and re-layouts  7.85 us (8%)
  other arithmetic  1.82 us (2%)
    all_gather x1, waiting for transfers between devices, per_device(): lax.all_gather(data, 'shot', axis=2, tiled=True)  62.6 us
    dot_general x4, matrix products, product(): jnp.einsum('jpy,jyu->jpu', left_factor, right_factor, preferred_element_t...  7.4 us
    slice x1, local copies, waits for them, and re-layouts, complex_block(): real_part = product(block[0], piece[0]) - product(block[1], piece[1])  3.21 us
  transfers between devices with their start and end apart: 1, of which 1 were waited for; matrix products, arithmetic and copies ran while one was open for 4% of the time, Pallas kernels for 0%

commit v1 on v0

v1 whole, which is shorter than its diff:
```python
import functools

import jax
import jax.numpy as jnp
from jax import lax
from jax.experimental import pallas as pl
from jax.experimental.pallas import tpu as pltpu
from jax.sharding import PartitionSpec as P

MESH = pl.DeviceIdType.MESH


def kernel(
    n, finish, data, aperture, ops, cable_ops, out,
    dbuf, apbuf, opsbuf, maskbuf, recv, maskrecv, send, back,
    local_sem, send_sem, recv_sem, mask_send_sem, mask_recv_sem, back_send_sem, back_recv_sem,
):
    me = lax.axis_index("shot")
    parts, freqs, shots, traces = data.shape
    mine = freqs // n
    total = n * shots
    cables = cable_ops.shape[0]
    width = ops.shape[1]

    barrier = pltpu.get_barrier_semaphore()

    def greet(i, carry):
        pl.semaphore_signal(barrier, inc=1, device_id={"shot": lax.rem(me + i, n)}, device_id_type=MESH)
        return carry

    lax.fori_loop(1, n, greet, 0)

    fetches = [
        pltpu.make_async_copy(aperture, apbuf, local_sem.at[0]),
        pltpu.make_async_copy(data, dbuf, local_sem.at[1]),
        pltpu.make_async_copy(ops, opsbuf, local_sem.at[2]),
    ]
    for fetch in fetches:
        fetch.start()

    fetches[0].wait()
    lists = apbuf[...]
    surface = lax.broadcasted_iota(jnp.int32, (shots, total), 1)
    found = jnp.zeros((shots, total), jnp.float32)
    for a in range(lists.shape[1]):
        found = jnp.where(lists[:, a : a + 1] == surface, 1.0, found)
    maskbuf[...] = found.astype(jnp.bfloat16)
    fetches[1].wait()
    fetches[2].wait()

    pl.semaphore_wait(barrier, n - 1)

    def scatter(i, carry):
        peer = lax.rem(me + i, n)
        pltpu.make_async_remote_copy(
            src_ref=maskbuf, dst_ref=maskrecv.at[me], send_sem=mask_send_sem, recv_sem=mask_recv_sem,
            device_id={"shot": peer}, device_id_type=MESH,
        ).start()
        pltpu.make_async_remote_copy(
            src_ref=dbuf.at[:, pl.ds(peer * mine, mine)], dst_ref=recv.at[me],
            send_sem=send_sem, recv_sem=recv_sem,
            device_id={"shot": peer}, device_id_type=MESH,
        ).start()
        return carry

    lax.fori_loop(1, n, scatter, 0)
    pltpu.make_async_copy(maskbuf, maskrecv.at[me], mask_recv_sem).start()
    pltpu.make_async_copy(dbuf.at[:, pl.ds(me * mine, mine)], recv.at[me], recv_sem).start()

    rows = []
    for c in range(cables):
        pieces = [jnp.zeros((width, width), jnp.float32)] * cables
        pieces[c] = opsbuf[cable_ops[c]].astype(jnp.float32)
        rows.append(jnp.concatenate(pieces, axis=1))
    operator = jnp.concatenate(rows, axis=0).astype(jnp.bfloat16)

    pltpu.make_async_copy(maskrecv, maskrecv, mask_recv_sem).wait()
    mask = maskrecv[...].astype(jnp.float32).reshape(total, total)
    pltpu.make_async_copy(recv, recv, recv_sem).wait()

    for f in range(mine):
        real = recv[:, 0, f].astype(jnp.float32).reshape(total, traces)
        imag = recv[:, 1, f].astype(jnp.float32).reshape(total, traces)
        left = jnp.concatenate([real * mask, imag * mask], axis=1).astype(jnp.bfloat16)
        right = jnp.concatenate(
            [jnp.concatenate([real, imag], axis=1), jnp.concatenate([-imag, real], axis=1)], axis=0
        ).astype(jnp.bfloat16)
        product = jnp.dot(left, right, preferred_element_type=jnp.float32)
        product = jnp.concatenate([product[:, :traces], product[:, traces:]], axis=0)
        high = product.astype(jnp.bfloat16)
        rest = product - high.astype(jnp.float32)
        middle = rest.astype(jnp.bfloat16)
        low = (rest - middle.astype(jnp.float32)).astype(jnp.bfloat16)
        result = jnp.dot(low, operator, preferred_element_type=jnp.float32)
        result += jnp.dot(middle, operator, preferred_element_type=jnp.float32)
        result += jnp.dot(high, operator, preferred_element_type=jnp.float32)
        result = result.reshape(parts, n, shots, traces)
        for p in range(parts):
            send[:, p, f] = result[p]

    def gather(i, carry):
        peer = lax.rem(me + i, n)
        pltpu.make_async_remote_copy(
            src_ref=send.at[peer], dst_ref=back.at[:, pl.ds(me * mine, mine)],
            send_sem=back_send_sem, recv_sem=back_recv_sem,
            device_id={"shot": peer}, device_id_type=MESH,
        ).start()
        return carry

    lax.fori_loop(1, n, gather, 0)
    pltpu.make_async_copy(send.at[me], back.at[:, pl.ds(me * mine, mine)], back_recv_sem).start()

    others = pl.ds(0, n - 1)
    pltpu.make_async_copy(maskrecv.at[others], maskrecv.at[others], mask_send_sem).wait()
    pltpu.make_async_copy(recv.at[others], recv.at[others], send_sem).wait()
    pltpu.make_async_copy(back, back, back_recv_sem).wait()
    if finish:
        predicted = back[...]
        energy = jnp.sum(jnp.sum(predicted * predicted, axis=(0, 1)), axis=1, keepdims=True)
        scale = lax.rsqrt(energy / (2.0 * freqs * traces) + 1e-06)
        out[...] = (predicted * scale[None, None]).astype(out.dtype)
    pltpu.make_async_copy(send.at[others], send.at[others], back_send_sem).wait()


def per_device(n, bands, data, aperture, ops, cable_ops):
    parts, freqs, shots, traces = data.shape
    mine = freqs // n
    finish = bands == 1
    dma = pltpu.SemaphoreType.DMA
    shape = (parts, freqs, shots, traces)
    scratch = [
        pltpu.VMEM(data.shape, data.dtype),
        pltpu.VMEM(aperture.shape, aperture.dtype),
        pltpu.VMEM(ops.shape, ops.dtype),
        pltpu.VMEM((shots, n * shots), jnp.bfloat16),
        pltpu.VMEM((n, parts, mine, shots, traces), jnp.bfloat16),
        pltpu.VMEM((n, shots, n * shots), jnp.bfloat16),
        pltpu.VMEM((n, parts, mine, shots, traces), jnp.float32),
    ]
    sems = [dma((3,))] + [dma] * 6
    anywhere = pl.BlockSpec(memory_space=pl.ANY)
    body = functools.partial(kernel, n, finish)
    if finish:
        scratch.append(pltpu.VMEM(shape, jnp.float32))
        out_dtype = jnp.bfloat16
    else:
        inner = body

        def body(data, aperture, ops, cable_ops, out, *rest):
            held = len(scratch)
            inner(data, aperture, ops, cable_ops, out, *rest[:held], out, *rest[held:])

        out_dtype = jnp.float32
    result = pl.pallas_call(
        body,
        out_shape=jax.ShapeDtypeStruct(shape, out_dtype),
        in_specs=[anywhere, anywhere, anywhere, pl.BlockSpec(memory_space=pltpu.SMEM)],
        out_specs=pl.BlockSpec(memory_space=pltpu.VMEM),
        scratch_shapes=scratch + sems,
        compiler_params=pltpu.CompilerParams(collective_id=0, has_side_effects=True),
        name="predict",
    )(data, aperture, ops, cable_ops)
    if finish:
        return result
    energy = lax.psum(jnp.sum(result * result, axis=(0, 1, 3)), "freq")
    scale = lax.rsqrt(energy / (2.0 * freqs * bands * traces) + 1e-06)
    return (result * scale[None, None, :, None]).astype(jnp.bfloat16)


def solution(mesh):
    return jax.shard_map(
        functools.partial(per_device, mesh.shape["shot"], mesh.shape["freq"]),
        mesh=mesh,
        in_specs=(P(None, "freq", "shot", None), P("shot", None), P(), P()),
        out_specs=P(None, "freq", "shot", None),
        check_vma=False,
    )
```

time: 96 us -> 22.5 us (0.23)
  the two profiles are of different devices: /device:TPU:0 before, /device:TPU:9 now
where the time goes in v1:
time: 22.5 us; the launch traced here: 22.4 us
  Pallas kernels  20.8 us (92%)
  local copies, waits for them, and re-layouts  1.61 us (7%)
    pallas_call x1, Pallas kernels, per_device(): pl.pallas_call(body, out_shape=jax.ShapeDtypeStruct(shape, out_dtype), in...  20.8 us
    unnamed x1, local copies, waits for them, and re-layouts  1.61 us

profile of v1, /device:TPU:9, one launch (start us, length us, event | category | flops | bytes accessed | tf_op | source)
XLA Modules:
  0.0 22.4 jit_solution(5049042488684090553)
XLA Ops:
  0.0 20.8 %predict.1 = bf16[2,64,4,128]{3,2,1,0:T(4,128)(2,1)} custom-call(bf16[2,64,4,128]{3,2,1,0:T(4,128)(2,1)} %data.1, s32[4,64]{1,0:T(4,128)} %aperture.1, bf16[8,64,64]{2,1,0:T(8,128)(2,1)} %ops.1, s32[2]{0:T(128)} %cable_ops.1), custom_call_target="tpu_custom_call" | custom-call | tf_op jit(solution)/shard_map/predict/pallas_call | solution.py:154
  20.8 1.6 %copy.6 = bf16[2,64,4,128]{3,2,1,0:T(4,128)(2,1)} copy(bf16[2,64,4,128]{3,2,1,0:T(4,128)(2,1)} %predict.1) | data formatting | bytes 262144

commit v2 on v1

v2 whole, which is shorter than its diff:
```python
import functools

import jax
import jax.numpy as jnp
from jax import lax
from jax.experimental import pallas as pl
from jax.experimental.pallas import tpu as pltpu
from jax.sharding import PartitionSpec as P

MESH = pl.DeviceIdType.MESH


def kernel(
    n, groups, chunks, finish, data, aperture, ops, cable_ops, out,
    dbuf, apbuf, opsbuf, maskbuf, recv, maskrecv, send, back,
    local_sem, recv_sem, send_sem, mask_send_sem, mask_recv_sem, back_send_sem, back_recv_sem,
):
    me = lax.axis_index("shot")
    parts, freqs, shots, traces = data.shape
    team = n // groups
    per = freqs // (team * chunks)
    total, rows = n * shots, team * shots
    cables = cable_ops.shape[0]
    width = ops.shape[1]
    seat = lax.rem(me, team)
    first = me - seat

    barrier = pltpu.get_barrier_semaphore()

    def greet(i, carry):
        pl.semaphore_signal(barrier, inc=1, device_id={"shot": lax.rem(me + i, n)}, device_id_type=MESH)
        return carry

    lax.fori_loop(1, n, greet, 0)

    fetches = [
        pltpu.make_async_copy(aperture, apbuf, local_sem.at[0]),
        pltpu.make_async_copy(data, dbuf, local_sem.at[1]),
        pltpu.make_async_copy(ops, opsbuf, local_sem.at[2]),
    ]
    for fetch in fetches:
        fetch.start()

    fetches[0].wait()
    lists = apbuf[...]
    surface = lax.broadcasted_iota(jnp.int32, (shots, total), 1)
    found = jnp.zeros((shots, total), jnp.float32)
    for a in range(lists.shape[1]):
        found = jnp.where(lists[:, a : a + 1] == surface, 1.0, found)
    maskbuf[...] = found.astype(jnp.bfloat16)
    fetches[1].wait()
    fetches[2].wait()

    pl.semaphore_wait(barrier, n - 1)

    def block(chunk, peer_seat):
        return dbuf.at[:, pl.ds((peer_seat * chunks + chunk) * per, per)]

    def team_peer(i):
        peer_seat = lax.rem(seat + i, team)
        return peer_seat, first + peer_seat

    def scatter(chunk, peer_seat, peer):
        pltpu.make_async_remote_copy(
            src_ref=block(chunk, peer_seat), dst_ref=recv.at[chunk, me],
            send_sem=send_sem, recv_sem=recv_sem.at[chunk],
            device_id={"shot": peer}, device_id_type=MESH,
        ).start()

    for chunk in range(chunks):

        def abroad(i, carry):
            peer_seat = lax.rem(seat + lax.rem(i, team), team)
            peer = lax.rem(first + team * (1 + i // team), n) + peer_seat
            scatter(chunk, peer_seat, peer)
            return carry

        def home(i, carry):
            peer_seat, peer = team_peer(i)
            if chunk == 0:
                pltpu.make_async_remote_copy(
                    src_ref=maskbuf, dst_ref=maskrecv.at[seat],
                    send_sem=mask_send_sem, recv_sem=mask_recv_sem,
                    device_id={"shot": peer}, device_id_type=MESH,
                ).start()
            scatter(chunk, peer_seat, peer)
            return carry

        lax.fori_loop(0, n - team, abroad, 0)
        lax.fori_loop(1, team, home, 0)
        if chunk == 0:
            pltpu.make_async_copy(maskbuf, maskrecv.at[seat], mask_recv_sem).start()
        pltpu.make_async_copy(block(chunk, seat), recv.at[chunk, me], recv_sem.at[chunk]).start()

    lines = []
    for c in range(cables):
        pieces = [jnp.zeros((width, width), jnp.float32)] * cables
        pieces[c] = opsbuf[cable_ops[c]].astype(jnp.float32)
        lines.append(jnp.concatenate(pieces, axis=1))
    operator = jnp.concatenate(lines, axis=0).astype(jnp.bfloat16)

    pltpu.make_async_copy(maskrecv, maskrecv, mask_recv_sem).wait()
    mask = maskrecv[...].astype(jnp.float32).reshape(rows, total)

    for chunk in range(chunks):
        pltpu.make_async_copy(recv.at[chunk], recv.at[chunk], recv_sem.at[chunk]).wait()
        for f in range(per):
            real = recv[chunk, :, 0, f].astype(jnp.float32).reshape(total, traces)
            imag = recv[chunk, :, 1, f].astype(jnp.float32).reshape(total, traces)
            if groups == 1:
                own_real, own_imag = real, imag
            else:
                own_real = recv[chunk, pl.ds(first, team), 0, f].astype(jnp.float32).reshape(rows, traces)
                own_imag = recv[chunk, pl.ds(first, team), 1, f].astype(jnp.float32).reshape(rows, traces)
            left = jnp.concatenate([own_real * mask, own_imag * mask], axis=1).astype(jnp.bfloat16)
            right = jnp.concatenate(
                [jnp.concatenate([real, imag], axis=1), jnp.concatenate([-imag, real], axis=1)], axis=0
            ).astype(jnp.bfloat16)
            product = jnp.dot(left, right, preferred_element_type=jnp.float32)
            product = jnp.concatenate([product[:, :traces], product[:, traces:]], axis=0)
            high = product.astype(jnp.bfloat16)
            rest = product - high.astype(jnp.float32)
            middle = rest.astype(jnp.bfloat16)
            low = (rest - middle.astype(jnp.float32)).astype(jnp.bfloat16)
            result = jnp.dot(low, operator, preferred_element_type=jnp.float32)
            result += jnp.dot(middle, operator, preferred_element_type=jnp.float32)
            result += jnp.dot(high, operator, preferred_element_type=jnp.float32)
            result = result.reshape(parts, team, shots, traces)
            for p in range(parts):
                send[chunk, :, p, f] = result[p]

        landing = back.at[:, pl.ds((seat * chunks + chunk) * per, per)]

        def gather(i, carry):
            peer_seat, peer = team_peer(i)
            pltpu.make_async_remote_copy(
                src_ref=send.at[chunk, peer_seat], dst_ref=landing,
                send_sem=back_send_sem, recv_sem=back_recv_sem,
                device_id={"shot": peer}, device_id_type=MESH,
            ).start()
            return carry

        lax.fori_loop(1, team, gather, 0)
        pltpu.make_async_copy(send.at[chunk, seat], landing, back_recv_sem).start()

    mask_sent = maskrecv.at[pl.ds(0, team - 1)]
    sent = recv.at[:, pl.ds(0, n - 1)]
    back_sent = send.at[:, pl.ds(0, team - 1)]
    pltpu.make_async_copy(mask_sent, mask_sent, mask_send_sem).wait()
    pltpu.make_async_copy(sent, sent, send_sem).wait()
    pltpu.make_async_copy(back, back, back_recv_sem).wait()
    if finish:
        predicted = back[...]
        energy = jnp.sum(jnp.sum(predicted * predicted, axis=(0, 1)), axis=1, keepdims=True)
        scale = lax.rsqrt(energy / (2.0 * freqs * traces) + 1e-06)
        out[...] = (predicted * scale[None, None]).astype(out.dtype)
    pltpu.make_async_copy(back_sent, back_sent, back_send_sem).wait()


GROUPS = 2
CHUNKS = 2


def per_device(n, bands, data, aperture, ops, cable_ops):
    parts, freqs, shots, traces = data.shape
    groups, chunks = GROUPS, CHUNKS
    team = n // groups
    per = freqs // (team * chunks)
    finish = bands == 1
    dma = pltpu.SemaphoreType.DMA
    shape = (parts, freqs, shots, traces)
    scratch = [
        pltpu.VMEM(data.shape, data.dtype),
        pltpu.VMEM(aperture.shape, aperture.dtype),
        pltpu.VMEM(ops.shape, ops.dtype),
        pltpu.VMEM((shots, n * shots), jnp.bfloat16),
        pltpu.VMEM((chunks, n, parts, per, shots, traces), jnp.bfloat16),
        pltpu.VMEM((team, shots, n * shots), jnp.bfloat16),
        pltpu.VMEM((chunks, team, parts, per, shots, traces), jnp.float32),
    ]
    sems = [dma((3,)), dma((chunks,))] + [dma] * 5
    anywhere = pl.BlockSpec(memory_space=pl.ANY)
    body = functools.partial(kernel, n, groups, chunks, finish)
    if finish:
        scratch.append(pltpu.VMEM(shape, jnp.float32))
        out_dtype = jnp.bfloat16
    else:
        inner = body

        def body(data, aperture, ops, cable_ops, out, *rest):
            held = len(scratch)
            inner(data, aperture, ops, cable_ops, out, *rest[:held], out, *rest[held:])

        out_dtype = jnp.float32
    result = pl.pallas_call(
        body,
        out_shape=jax.ShapeDtypeStruct(shape, out_dtype),
        in_specs=[anywhere, anywhere, anywhere, pl.BlockSpec(memory_space=pltpu.SMEM)],
        out_specs=pl.BlockSpec(memory_space=pltpu.VMEM),
        scratch_shapes=scratch + sems,
        compiler_params=pltpu.CompilerParams(collective_id=0, has_side_effects=True),
        name="predict",
    )(data, aperture, ops, cable_ops)
    if finish:
        return result
    energy = lax.psum(jnp.sum(result * result, axis=(0, 1, 3)), "freq")
    scale = lax.rsqrt(energy / (2.0 * freqs * bands * traces) + 1e-06)
    return (result * scale[None, None, :, None]).astype(jnp.bfloat16)


def solution(mesh):
    return jax.shard_map(
        functools.partial(per_device, mesh.shape["shot"], mesh.shape["freq"]),
        mesh=mesh,
        in_specs=(P(None, "freq", "shot", None), P("shot", None), P(), P()),
        out_specs=P(None, "freq", "shot", None),
        check_vma=False,
    )
```

time: 22.5 us -> 22.3 us (level)
  the two profiles are of different devices: /device:TPU:9 before, /device:TPU:0 now
where the time goes in v2:
time: 22.3 us; the launch traced here: 22.2 us
  Pallas kernels  20.5 us (92%)
  local copies, waits for them, and re-layouts  1.61 us (7%)
    pallas_call x1, Pallas kernels, per_device(): pl.pallas_call(body, out_shape=jax.ShapeDtypeStruct(shape, out_dtype), in...  20.5 us
    unnamed x1, local copies, waits for them, and re-layouts  1.61 us

profile of v2, /device:TPU:0, one launch (start us, length us, event | category | flops | bytes accessed | tf_op | source)
XLA Modules:
  0.0 22.2 jit_solution(7822067623916329845)
XLA Ops:
  0.0 20.5 %predict.1 = bf16[2,64,4,128]{3,2,1,0:T(4,128)(2,1)} custom-call(bf16[2,64,4,128]{3,2,1,0:T(4,128)(2,1)} %data.1, s32[4,64]{1,0:T(4,128)} %aperture.1, bf16[8,64,64]{2,1,0:T(8,128)(2,1)} %ops.1, s32[2]{0:T(128)} %cable_ops.1), custom_call_target="tpu_custom_call" | custom-call | tf_op jit(solution)/shard_map/predict/pallas_call | solution.py:195
  20.6 1.6 %copy.6 = bf16[2,64,4,128]{3,2,1,0:T(4,128)(2,1)} copy(bf16[2,64,4,128]{3,2,1,0:T(4,128)(2,1)} %predict.1) | data formatting | bytes 262144

commit v3 on v2

--- a/solution.py
+++ b/solution.py
@@ -13,31 +13,36 @@
 def kernel(
     n, groups, chunks, finish, data, aperture, ops, cable_ops, out,
     dbuf, apbuf, opsbuf, maskbuf, recv, maskrecv, send, back,
-    local_sem, recv_sem, send_sem, mask_send_sem, mask_recv_sem, back_send_sem, back_recv_sem,
+    local_sem, recv_sem, send_sem, mask_send_sem, mask_recv_sem, back_send_sem, back_recv_sem, team_sem,
 ):
     me = lax.axis_index("shot")
-    parts, freqs, shots, traces = data.shape
+    parts, blocks, per, shots, traces = data.shape
     team = n // groups
-    per = freqs // (team * chunks)
+    freqs = blocks * per
     total, rows = n * shots, team * shots
     cables = cable_ops.shape[0]
     width = ops.shape[1]
     seat = lax.rem(me, team)
     first = me - seat
 
+    flips = []
+    for place in (1 << k for k in range(n.bit_length() - 1)):
+        flips.append((place, place * (1 - 2 * lax.rem(me // place, 2))))
+
+    def partner(m):
+        return me + sum(flip for place, flip in flips if m & place)
+
+    def partner_seat(m):
+        return seat + sum(flip for place, flip in flips if m & place and place < team)
+
     barrier = pltpu.get_barrier_semaphore()
-
-    def greet(i, carry):
-        pl.semaphore_signal(barrier, inc=1, device_id={"shot": lax.rem(me + i, n)}, device_id_type=MESH)
-        return carry
-
-    lax.fori_loop(1, n, greet, 0)
+    for m in reversed(range(team, n)):
+        pl.semaphore_signal(barrier, inc=1, device_id={"shot": partner(m)}, device_id_type=MESH)
 
     fetches = [
         pltpu.make_async_copy(aperture, apbuf, local_sem.at[0]),
-        pltpu.make_async_copy(data, dbuf, local_sem.at[1]),
-        pltpu.make_async_copy(ops, opsbuf, local_sem.at[2]),
-    ]
+        pltpu.make_async_copy(ops, opsbuf, local_sem.at[1]),
+    ] + [pltpu.make_async_copy(data.at[p], dbuf.at[:, p], local_sem.at[2 + p]) for p in range(parts)]
     for fetch in fetches:
         fetch.start()
 
@@ -48,17 +53,14 @@
     for a in range(lists.shape[1]):
         found = jnp.where(lists[:, a : a + 1] == surface, 1.0, found)
     maskbuf[...] = found.astype(jnp.bfloat16)
-    fetches[1].wait()
-    fetches[2].wait()
-
-    pl.semaphore_wait(barrier, n - 1)
+    for fetch in fetches[1:]:
+        fetch.wait()
+
+    pl.semaphore_wait(barrier, n - team)
+    pl.semaphore_signal(team_sem, inc=1, device_id={"shot": partner(team)}, device_id_type=MESH)
 
     def block(chunk, peer_seat):
-        return dbuf.at[:, pl.ds((peer_seat * chunks + chunk) * per, per)]
-
-    def team_peer(i):
-        peer_seat = lax.rem(seat + i, team)
-        return peer_seat, first + peer_seat
+        return dbuf.at[peer_seat * chunks + chunk]
 
     def scatter(chunk, peer_seat, peer):
         pltpu.make_async_remote_copy(
@@ -68,26 +70,16 @@
         ).start()
 
     for chunk in range(chunks):
-
-        def abroad(i, carry):
-            peer_seat = lax.rem(seat + lax.rem(i, team), team)
-            peer = lax.rem(first + team * (1 + i // team), n) + peer_seat
-            scatter(chunk, peer_seat, peer)
-            return carry
-
-        def home(i, carry):
-            peer_seat, peer = team_peer(i)
-            if chunk == 0:
+        for m in reversed(range(1, n)):
+            if chunk == 0 and m == team - 1:
+                pl.semaphore_wait(team_sem, 1)
+            if chunk == 0 and m < team:
                 pltpu.make_async_remote_copy(
                     src_ref=maskbuf, dst_ref=maskrecv.at[seat],
                     send_sem=mask_send_sem, recv_sem=mask_recv_sem,
-                    device_id={"shot": peer}, device_id_type=MESH,
+                    device_id={"shot": partner(m)}, device_id_type=MESH,
                 ).start()
-            scatter(chunk, peer_seat, peer)
-            return carry
-
-        lax.fori_loop(0, n - team, abroad, 0)
-        lax.fori_loop(1, team, home, 0)
+            scatter(chunk, partner_seat(m), partner(m))
         if chunk == 0:
             pltpu.make_async_copy(maskbuf, maskrecv.at[seat], mask_recv_sem).start()
         pltpu.make_async_copy(block(chunk, seat), recv.at[chunk, me], recv_sem.at[chunk]).start()
@@ -129,18 +121,14 @@
             for p in range(parts):
                 send[chunk, :, p, f] = result[p]
 
-        landing = back.at[:, pl.ds((seat * chunks + chunk) * per, per)]
-
-        def gather(i, carry):
-            peer_seat, peer = team_peer(i)
+        landing = back.at[seat * chunks + chunk]
+
+        for m in reversed(range(1, team)):
             pltpu.make_async_remote_copy(
-                src_ref=send.at[chunk, peer_seat], dst_ref=landing,
+                src_ref=send.at[chunk, partner_seat(m)], dst_ref=landing,
                 send_sem=back_send_sem, recv_sem=back_recv_sem,
-                device_id={"shot": peer}, device_id_type=MESH,
+                device_id={"shot": partner(m)}, device_id_type=MESH,
             ).start()
-            return carry
-
-        lax.fori_loop(1, team, gather, 0)
         pltpu.make_async_copy(send.at[chunk, seat], landing, back_recv_sem).start()
 
     mask_sent = maskrecv.at[pl.ds(0, team - 1)]
@@ -151,9 +139,10 @@
     pltpu.make_async_copy(back, back, back_recv_sem).wait()
     if finish:
         predicted = back[...]
-        energy = jnp.sum(jnp.sum(predicted * predicted, axis=(0, 1)), axis=1, keepdims=True)
+        energy = jnp.sum(jnp.sum(predicted * predicted, axis=(0, 1, 2)), axis=1, keepdims=True)
         scale = lax.rsqrt(energy / (2.0 * freqs * traces) + 1e-06)
-        out[...] = (predicted * scale[None, None]).astype(out.dtype)
+        for p in range(parts):
+            out[p] = (back[:, p] * scale[None, None]).astype(out.dtype)
     pltpu.make_async_copy(back_sent, back_sent, back_send_sem).wait()
 
 
@@ -168,9 +157,11 @@
     per = freqs // (team * chunks)
     finish = bands == 1
     dma = pltpu.SemaphoreType.DMA
-    shape = (parts, freqs, shots, traces)
+    blocks = team * chunks
+    held = (blocks, parts, per, shots, traces)
+    shape = (parts, blocks, per, shots, traces) if finish else held
     scratch = [
-        pltpu.VMEM(data.shape, data.dtype),
+        pltpu.VMEM(held, data.dtype),
         pltpu.VMEM(aperture.shape, aperture.dtype),
         pltpu.VMEM(ops.shape, ops.dtype),
         pltpu.VMEM((shots, n * shots), jnp.bfloat16),
@@ -178,18 +169,18 @@
         pltpu.VMEM((team, shots, n * shots), jnp.bfloat16),
         pltpu.VMEM((chunks, team, parts, per, shots, traces), jnp.float32),
     ]
-    sems = [dma((3,)), dma((chunks,))] + [dma] * 5
+    sems = [dma((2 + parts,)), dma((chunks,))] + [dma] * 5 + [pltpu.SemaphoreType.REGULAR]
     anywhere = pl.BlockSpec(memory_space=pl.ANY)
     body = functools.partial(kernel, n, groups, chunks, finish)
     if finish:
-        scratch.append(pltpu.VMEM(shape, jnp.float32))
+        scratch.append(pltpu.VMEM(held, jnp.float32))
         out_dtype = jnp.bfloat16
     else:
         inner = body
 
         def body(data, aperture, ops, cable_ops, out, *rest):
-            held = len(scratch)
-            inner(data, aperture, ops, cable_ops, out, *rest[:held], out, *rest[held:])
+            place = len(scratch)
+            inner(data, aperture, ops, cable_ops, out, *rest[:place], out, *rest[place:])
 
         out_dtype = jnp.float32
     result = pl.pallas_call(
@@ -200,9 +191,10 @@
         scratch_shapes=scratch + sems,
         compiler_params=pltpu.CompilerParams(collective_id=0, has_side_effects=True),
         name="predict",
-    )(data, aperture, ops, cable_ops)
+    )(data.reshape(parts, blocks, per, shots, traces), aperture, ops, cable_ops)
     if finish:
-        return result
+        return result.reshape(data.shape)
+    result = jnp.swapaxes(result, 0, 1).reshape(data.shape)
     energy = lax.psum(jnp.sum(result * result, axis=(0, 1, 3)), "freq")
     scale = lax.rsqrt(energy / (2.0 * freqs * bands * traces) + 1e-06)
     return (result * scale[None, None, :, None]).astype(jnp.bfloat16)

time: 22.3 us -> 21.6 us (0.969)
  Pallas kernels: 20.5 us -> 19.8 us
    pallas_call x1, Pallas kernels: 20.5 us -> 19.8 us  [per_device(): pl.pallas_call(body, out_shape=jax.ShapeDtypeStruct(shape, out_dtype), in...]
where the time goes in v3:
time: 21.6 us; the launch traced here: 21.4 us
  Pallas kernels  19.8 us (92%)
  local copies, waits for them, and re-layouts  1.61 us (7%)
    pallas_call x1, Pallas kernels, per_device(): pl.pallas_call(body, out_shape=jax.ShapeDtypeStruct(shape, out_dtype), in...  19.8 us
    unnamed x1, local copies, waits for them, and re-layouts  1.61 us

profile of v3, /device:TPU:0, one launch (start us, length us, event | category | flops | bytes accessed | tf_op | source)
XLA Modules:
  0.0 21.4 jit_solution(13651644208102085448)
XLA Ops:
  0.0 19.8 %predict.1 = bf16[2,32,2,4,128]{4,3,2,1,0:T(4,128)(2,1)} custom-call(bf16[2,32,2,4,128]{4,3,2,1,0:T(4,128)(2,1)} %bitcast.3, s32[4,64]{1,0:T(4,128)} %aperture.1, bf16[8,64,64]{2,1,0:T(8,128)(2,1)} %ops.1, s32[2]{0:T(128)} %cable_ops.1), custom_call_target="tpu_custom_call" | custom-call | tf_op jit(solution)/shard_map/predict/pallas_call | solution.py:186
  19.8 1.6 %copy.6 = bf16[2,64,4,128]{3,2,1,0:T(4,128)(2,1)} copy(bf16[2,64,4,128]{3,2,1,0:T(4,128)(2,1)} %bitcast.2) | data formatting | bytes 262144

commit v4 on v3

--- a/solution.py
+++ b/solution.py
@@ -185,7 +185,7 @@
         out_dtype = jnp.float32
     result = pl.pallas_call(
         body,
-        out_shape=jax.ShapeDtypeStruct(shape, out_dtype),
+        out_shape=pltpu.VMEM(shape, out_dtype),
         in_specs=[anywhere, anywhere, anywhere, pl.BlockSpec(memory_space=pltpu.SMEM)],
         out_specs=pl.BlockSpec(memory_space=pltpu.VMEM),
         scratch_shapes=scratch + sems,

time: 21.6 us -> 20 us (0.926)
  local copies, waits for them, and re-layouts: 1.61 us -> 0.66 us
  Pallas kernels: 19.8 us -> 19.2 us
    unnamed x1, local copies, waits for them, and re-layouts: 1.61 us -> 0.66 us
    pallas_call x1, Pallas kernels: 19.8 us -> 19.2 us  [per_device(): pl.pallas_call(body, out_shape=pltpu.VMEM(shape, out_dtype), in_specs=[an...]
where the time goes in v4:
time: 20 us; the launch traced here: 19.8 us
  Pallas kernels  19.2 us (96%)
  local copies, waits for them, and re-layouts  0.66 us (3%)
    pallas_call x1, Pallas kernels, per_device(): pl.pallas_call(body, out_shape=pltpu.VMEM(shape, out_dtype), in_specs=[an...  19.2 us
    unnamed x1, local copies, waits for them, and re-layouts  0.66 us

profile of v4, /device:TPU:0, one launch (start us, length us, event | category | flops | bytes accessed | tf_op | source)
XLA Modules:
  0.0 19.8 jit_solution(4898600149520176689)
XLA Ops:
  0.0 19.2 %predict.1 = bf16[2,32,2,4,128]{4,3,2,1,0:T(4,128)(2,1)S(1)} custom-call(bf16[2,32,2,4,128]{4,3,2,1,0:T(4,128)(2,1)} %bitcast.3, s32[4,64]{1,0:T(4,128)} %aperture.1, bf16[8,64,64]{2,1,0:T(8,128)(2,1)} %ops.1, s32[2]{0:T(128)} %cable_ops.1), custom_call_target="tpu_custom_call" | custom-call | tf_op jit(solution)/shard_map/predict/pallas_call | solution.py:186
  19.2 0.7 %copy.6 = bf16[2,64,4,128]{3,2,1,0:T(4,128)(2,1)} copy(bf16[2,64,4,128]{3,2,1,0:T(4,128)(2,1)S(1)} %bitcast.2) | data formatting | bytes 262144

commit v5 on v4

--- a/solution.py
+++ b/solution.py
@@ -12,7 +12,7 @@
 
 def kernel(
     n, groups, chunks, finish, data, aperture, ops, cable_ops, out,
-    dbuf, apbuf, opsbuf, maskbuf, recv, maskrecv, send, back,
+    dbuf, apbuf, opsbuf, idbuf, maskbuf, recv, maskrecv, send, back,
     local_sem, recv_sem, send_sem, mask_send_sem, mask_recv_sem, back_send_sem, back_recv_sem, team_sem,
 ):
     me = lax.axis_index("shot")
@@ -43,6 +43,7 @@
         pltpu.make_async_copy(aperture, apbuf, local_sem.at[0]),
         pltpu.make_async_copy(ops, opsbuf, local_sem.at[1]),
     ] + [pltpu.make_async_copy(data.at[p], dbuf.at[:, p], local_sem.at[2 + p]) for p in range(parts)]
+    fetches.append(pltpu.make_async_copy(cable_ops, idbuf, local_sem.at[2 + parts]))
     for fetch in fetches:
         fetch.start()
 
@@ -87,7 +88,7 @@
     lines = []
     for c in range(cables):
         pieces = [jnp.zeros((width, width), jnp.float32)] * cables
-        pieces[c] = opsbuf[cable_ops[c]].astype(jnp.float32)
+        pieces[c] = opsbuf[idbuf[c]].astype(jnp.float32)
         lines.append(jnp.concatenate(pieces, axis=1))
     operator = jnp.concatenate(lines, axis=0).astype(jnp.bfloat16)
 
@@ -164,12 +165,13 @@
         pltpu.VMEM(held, data.dtype),
         pltpu.VMEM(aperture.shape, aperture.dtype),
         pltpu.VMEM(ops.shape, ops.dtype),
+        pltpu.SMEM(cable_ops.shape, cable_ops.dtype),
         pltpu.VMEM((shots, n * shots), jnp.bfloat16),
         pltpu.VMEM((chunks, n, parts, per, shots, traces), jnp.bfloat16),
         pltpu.VMEM((team, shots, n * shots), jnp.bfloat16),
         pltpu.VMEM((chunks, team, parts, per, shots, traces), jnp.float32),
     ]
-    sems = [dma((2 + parts,)), dma((chunks,))] + [dma] * 5 + [pltpu.SemaphoreType.REGULAR]
+    sems = [dma((3 + parts,)), dma((chunks,))] + [dma] * 5 + [pltpu.SemaphoreType.REGULAR]
     anywhere = pl.BlockSpec(memory_space=pl.ANY)
     body = functools.partial(kernel, n, groups, chunks, finish)
     if finish:
@@ -186,7 +188,7 @@
     result = pl.pallas_call(
         body,
         out_shape=pltpu.VMEM(shape, out_dtype),
-        in_specs=[anywhere, anywhere, anywhere, pl.BlockSpec(memory_space=pltpu.SMEM)],
+        in_specs=[anywhere] * 4,
         out_specs=pl.BlockSpec(memory_space=pltpu.VMEM),
         scratch_shapes=scratch + sems,
         compiler_params=pltpu.CompilerParams(collective_id=0, has_side_effects=True),

time: 20 us -> 19.4 us (0.970)
  Pallas kernels: 19.2 us -> 18.6 us
    pallas_call x1, Pallas kernels: 19.2 us -> 18.6 us  [per_device(): pl.pallas_call(body, out_shape=pltpu.VMEM(shape, out_dtype), in_specs=[an...]
where the time goes in v5:
time: 19.4 us; the launch traced here: 19.2 us
  Pallas kernels  18.6 us (96%)
  local copies, waits for them, and re-layouts  0.66 us (3%)
    pallas_call x1, Pallas kernels, per_device(): pl.pallas_call(body, out_shape=pltpu.VMEM(shape, out_dtype), in_specs=[an...  18.6 us
    unnamed x1, local copies, waits for them, and re-layouts  0.66 us

profile of v5, /device:TPU:0, one launch (start us, length us, event | category | flops | bytes accessed | tf_op | source)
XLA Modules:
  0.0 19.2 jit_solution(16090755319827850833)
XLA Ops:
  0.0 18.6 %predict.1 = bf16[2,32,2,4,128]{4,3,2,1,0:T(4,128)(2,1)S(1)} custom-call(bf16[2,32,2,4,128]{4,3,2,1,0:T(4,128)(2,1)} %bitcast.3, s32[4,64]{1,0:T(4,128)} %aperture.1, bf16[8,64,64]{2,1,0:T(8,128)(2,1)} %ops.1, s32[2]{0:T(128)} %cable_ops.1), custom_call_target="tpu_custom_call" | custom-call | tf_op jit(solution)/shard_map/predict/pallas_call | solution.py:188
  18.6 0.7 %copy.6 = bf16[2,64,4,128]{3,2,1,0:T(4,128)(2,1)} copy(bf16[2,64,4,128]{3,2,1,0:T(4,128)(2,1)S(1)} %bitcast.2) | data formatting | bytes 262144
